TPU v7x, 256 devices: a whole 4x4x8 slice. The times are simulated.
256 devices in a mesh: section: 4 (over x), dp: 4 (over y), chan: 16 (over z, core).
Axes of the slice: x: 4, y: 4, z: 8, core: 2. Of those that a mesh axis runs over, the one named last changes fastest.
Arguments:
- feats: bfloat16 [8, 32, 128, 2048], P('dp', None, None, 'chan'), may hold values from -6 to 6
- offsets: int32 [8], P('dp'), may hold values from 0 to 127
- widths: int32 [8], P('dp'), may hold values from 32 to 64
- labels: int32 [8, 32, 128], P('dp'), may hold values from 0 to 19
- dw_kernel: bfloat16 [4, 9, 2048], P('section', None, 'chan'), may hold values from -2 to 2
- pw_weight: bfloat16 [4, 2048, 256], P('section', 'chan'), may hold values from -0.125 to 0.125
- pw_bias: float32 [4, 256], P('section', 'chan'), may hold values from -3 to 3
- proj: bfloat16 [4, 256, 256], P('section', 'chan'), may hold values from -0.1875 to 0.1875
- proj_bias: float32 [256], P('chan'), may hold values from -3 to 3
- upstream: bfloat16 [256, 8, 32, 128], P('chan', 'dp'), may hold values from -6 to 6
Outputs:
- aspp_out: bfloat16 [256, 8, 32, 128], P('chan', 'dp')
- input_grad: bfloat16 [8, 32, 128, 2048], P('dp', 'section', None, 'chan')
- grad_dw: float32 [4, 9, 2048], P('section', None, 'chan')
- grad_pw: float32 [4, 2048, 256], P('section', 'chan')
- grad_pw_bias: float32 [4, 256], P('section', 'chan')
- grad_proj: float32 [4, 256, 256], P('section', 'chan')
- grad_proj_bias: float32 [256], P('chan')
All inputs are finite; a program needn't handle non-finite values.
Results may differ from a plain program's by a relative error of at most 0.008.
Values may be sent and summed in bfloat16 or wider, within the bound.
No kernel may reach another device: no remote copies, remote signals or barrier semaphores. Data moves between devices by JAX's collectives and lax.ppermute only.
A program may use at most 128 MiB of HBM per device.

v0:
```python
import math
import jax
import jax.numpy as jnp
from jax import lax
from jax.sharding import PartitionSpec as P

RATE = 6
void_class = 19


def prefix(shard, axis, combine, identity):
    devices, place = (lax.axis_size(axis), lax.axis_index(axis))
    everything = lax.all_gather(shard, axis)
    start = jnp.broadcast_to(jnp.asarray(identity, shard.dtype), shard.shape)

    def step(k, before):
        reached = k < place
        new = combine(before, everything[k])
        return jnp.where(reached, new, before)

    return lax.fori_loop(0, devices, step, start)


def spread(value, axis, source):
    kept = jnp.where(lax.axis_index(axis) == source, value, 0).astype(value.dtype)
    return lax.psum(kept, axis)


def column_band(offsets, widths, col_count):
    columns = jnp.arange(col_count, dtype=jnp.int32)
    return jnp.mod(columns[None, :] - offsets[:, None], col_count) < widths[:, None]


def swish_slope(value):
    sig = jax.nn.sigmoid(value)
    return sig * (1.0 + value * (1.0 - sig))


def add_terms(earlier, latter):
    return earlier + latter


def local(feats, offsets, widths, labels, dw_kernel, pw_weight, pw_bias, proj, proj_bias, upstream):
    frame_count, row_count, col_count, chan_count = feats.shape
    segments = lax.axis_size("section")
    dilation = RATE * lax.axis_index("section")
    margin = RATE * (segments - 1)
    keep = column_band(offsets, widths, col_count)
    masked = feats * keep[:, None, :, None].astype(jnp.bfloat16)
    padded = jnp.pad(masked, ((0, 0), (margin, margin), (margin, margin), (0, 0)))
    kernel = dw_kernel[0].astype(jnp.float32)
    pixel_count = frame_count * row_count * col_count
    scaling = 1.0 / math.sqrt(pixel_count * lax.axis_size("dp"))

    def tap_slice(source, tap_index, direction):
        row_step = tap_index // 3 - 1
        col_step = tap_index % 3 - 1
        anchor = (
            0,
            margin + direction * dilation * row_step,
            margin + direction * dilation * col_step,
            0,
        )
        return lax.dynamic_slice(source, anchor, (frame_count, row_count, col_count, chan_count))

    accum = jnp.zeros((frame_count, row_count, col_count, chan_count), jnp.float32)
    for tap_index in range(9):
        accum = accum + tap_slice(padded, tap_index, 1).astype(jnp.float32) * kernel[tap_index]
    depth_out = accum.astype(jnp.bfloat16)
    depth_rows = depth_out.reshape(pixel_count, chan_count)
    weight = pw_weight[0]
    branch_share = pw_bias.shape[1]
    columns = weight
    preact = (
        lax.psum_scatter(
            lax.dot_general(
                columns, depth_rows, (((0,), (1,)), ((), ())), preferred_element_type=jnp.float32
            ),
            "chan",
            scatter_dimension=0,
            tiled=True,
        )
        + pw_bias[0][:, None]
    )
    branch_act = jax.nn.silu(preact).astype(jnp.bfloat16)
    proj_local = proj[0]
    columns = proj_local
    zpart = lax.psum_scatter(
        lax.dot_general(
            columns, branch_act, (((0,), (0,)), ((), ())), preferred_element_type=jnp.float32
        ),
        "chan",
        scatter_dimension=0,
        tiled=True,
    )
    up_rows = upstream.reshape(branch_share, pixel_count).astype(jnp.float32)
    labeled = (labels != void_class).reshape(pixel_count).astype(jnp.float32)
    before = prefix(zpart, "section", add_terms, jnp.zeros_like(zpart))
    zvalue = before + zpart + proj_bias[:, None]
    result = jax.nn.silu(zvalue).astype(jnp.bfloat16)
    gradient = (up_rows * swish_slope(zvalue) * labeled[None, :]).astype(jnp.bfloat16)
    result, out_grad = (result, gradient)
    result, out_grad = (
        spread(result, "section", segments - 1),
        spread(out_grad, "section", segments - 1),
    )
    proj_bias_grad = jnp.sum(out_grad.astype(jnp.float32), axis=1) * scaling
    shard_rows = lax.all_gather(out_grad, "chan", axis=0, tiled=True)
    act_grad = jnp.dot(proj_local, shard_rows, preferred_element_type=jnp.float32)
    piece_grad = lax.dot_general(
        branch_act, shard_rows, (((1,), (1,)), ((), ())), preferred_element_type=jnp.float32
    )
    proj_grad = piece_grad
    act_grad, proj_grad = (act_grad, proj_grad)
    pre_grad = (act_grad * swish_slope(preact)).astype(jnp.bfloat16)
    pw_bias_grad = jnp.sum(pre_grad.astype(jnp.float32), axis=1) * scaling
    shard_rows = lax.all_gather(pre_grad, "chan", axis=0, tiled=True)
    columns = weight
    depth_acc = lax.dot_general(
        shard_rows, columns, (((0,), (1,)), ((), ())), preferred_element_type=jnp.float32
    )
    piece_grad = lax.dot_general(
        depth_rows, shard_rows, (((0,), (1,)), ((), ())), preferred_element_type=jnp.float32
    )
    weight_grad = piece_grad
    depth_acc, weight_grad = (depth_acc, weight_grad)
    depth_grad = depth_acc.astype(jnp.bfloat16).reshape(
        frame_count, row_count, col_count, chan_count
    )
    padded_grad = jnp.pad(depth_grad, ((0, 0), (margin, margin), (margin, margin), (0, 0)))
    depth_f = depth_grad.astype(jnp.float32)
    input_term = jnp.zeros((frame_count, row_count, col_count, chan_count), jnp.float32)
    tap_grads = []
    for tap_index in range(9):
        source = tap_slice(padded, tap_index, 1).astype(jnp.float32)
        tap_grads.append(jnp.sum(source * depth_f, axis=(0, 1, 2)) * scaling)
        input_term = (
            input_term
            + tap_slice(padded_grad, tap_index, -1).astype(jnp.float32) * kernel[tap_index]
        )
    kernel_grad = jnp.stack(tap_grads)
    input_rows = lax.psum_scatter(input_term, "section", scatter_dimension=1, tiled=True)
    input_grad = (input_rows * keep[:, None, :, None].astype(jnp.float32)).astype(jnp.bfloat16)
    kernel_grad, weight_grad, pw_bias_grad, proj_grad, proj_bias_grad = lax.psum(
        (kernel_grad, weight_grad * scaling, pw_bias_grad, proj_grad * scaling, proj_bias_grad),
        "dp",
    )
    aspp_out = result.reshape(branch_share, frame_count, row_count, col_count)
    return (
        aspp_out,
        input_grad,
        kernel_grad[None],
        weight_grad[None],
        pw_bias_grad[None],
        proj_grad[None],
        proj_bias_grad,
    )


def solution(mesh):
    in_specs = (
        P("dp", None, None, "chan"),
        P("dp"),
        P("dp"),
        P("dp", None, None),
        P("section", None, "chan"),
        P("section", "chan", None),
        P("section", "chan"),
        P("section", "chan", None),
        P("chan"),
        P("chan", "dp", None, None),
    )
    out_specs = (
        P("chan", "dp", None, None),
        P("dp", "section", None, "chan"),
        P("section", None, "chan"),
        P("section", "chan", None),
        P("section", "chan"),
        P("section", "chan", None),
        P("chan"),
    )
    return jax.shard_map(local, mesh=mesh, in_specs=in_specs, out_specs=out_specs, check_vma=False)
```

profile of v0, /device:TPU:2, one launch (start us, length us, event | category | flops | bytes accessed | tf_op | source)
XLA Modules:
  0.0 520.5 jit_solution(6234613447369685872)
XLA Ops:
  7.2 0.0 reduce-scatter.11.cloned.1.call-start
  7.2 0.7 convert_element_type.135
  7.9 0.7 fusion.36
  8.7 1.8 broadcast_multiply_fusion
  10.5 1.3 copy-done.1
  11.8 16.0 %fusion.10 = bf16[2,32,128,128]{3,2,1,0:T(8,128)(2,1)S(1)} fusion(bf16[2,32,128,128]{3,2,1,0:T(8,128)(2,1)S(1)} %broadcast_multiply_fusion, f32[128]{0:T(128)S(1)} %get-tuple-element.153, f32[128]{0:T(128)S(1)} %get-tuple-element.154, f32[128]{0:T(128)S(1)} %get-tuple-element.155, f32[128]{0:T(128)S(1)} %get-tuple-element.156, ...), kind=kLoop, calls=%fused_computation.50 | loop fusion | flops 28311552 | bytes 4198928 | tf_op jit(solution)/shard_map/convert_element_type | solution.py:69
  27.8 4.5 convolution_bitcast_fusion.1
  32.3 8.9 %copy.33 = f32[256,8192]{1,0:T(8,128)} copy(f32[256,8192]{0,1:T(8,128)} %convolution_bitcast_fusion.1) | data formatting | bytes 16777216
  41.2 0.2 reduce-scatter.13.cloned.1.call-start
  41.5 73.4 %reduce-scatter.11.cloned.1.call-done = f32[16,8192]{1,0:T(8,128)} async-done(((f32[256,8192]{1,0:T(8,128)}), f32[16,8192]{1,0:T(8,128)}) %reduce-scatter.11.cloned.1.call-update) | async-done | bytes 524304 | tf_op jit(solution)/shard_map/reduce_scatter | solution.py:75
  114.9 5.6 %convolution_bitcast_fusion = f32[256,8192]{0,1:T(8,128)} fusion(bf16[1,16,256]{2,1,0:T(8,128)(2,1)S(1)} %copy-done.7, f32[16,8192]{1,0:T(8,128)} %reduce-scatter.11.cloned.1.call-done, f32[16]{0:T(128)S(1)} %bitcast.133), kind=kOutput, calls=%fused_computation.27 | convolution fusion | flops 67895296 | bytes 8921152 | tf_op jit(solution)/shard_map/dot_general | solution.py:89
  120.6 8.9 %copy.35 = f32[256,8192]{1,0:T(8,128)} copy(f32[256,8192]{0,1:T(8,128)} %convolution_bitcast_fusion) | data formatting | bytes 16777216
  129.5 0.0 all-gather.9.cloned.1.call-start
  129.6 69.4 %reduce-scatter.13.cloned.1.call-done = f32[16,8192]{1,0:T(8,128)} async-done(((f32[256,8192]{1,0:T(8,128)}), f32[16,8192]{1,0:T(8,128)}) %reduce-scatter.13.cloned.1.call-update) | async-done | bytes 524304 | tf_op jit(solution)/shard_map/reduce_scatter | solution.py:88
  199.0 0.0 all-reduce.9.cloned.1.call-start
  199.0 0.8 convert.2
  199.9 32.1 %all-gather.9.cloned.1.call-done = f32[64,8192]{1,0:T(8,128)} async-done(((f32[16,8192]{1,0:T(8,128)}), f32[64,8192]{1,0:T(8,128)}) %all-gather.9.cloned.1.call-update) | async-done | bytes 2097168 | tf_op jit(solution)/shard_map/all_gather | solution.py:13
  232.0 4.9 while.14
  232.0 1.3 add_select_fusion.2
  233.3 1.2 add_select_fusion.2
  234.5 1.2 add_select_fusion.2
  235.7 1.2 add_select_fusion.2
  236.9 2.4 broadcast_select_fusion
  239.3 0.8 copy.39
  240.1 0.0 all-gather.5.cloned.1.call-start
  240.2 48.3 %all-reduce.9.cloned.1.call-done = (bf16[16,2,32,128]{3,2,1,0:T(8,128)(2,1)}, bf16[16,8192]{1,0:T(8,128)(2,1)}) async-done(((bf16[16,2,32,128]{3,2,1,0:T(8,128)(2,1)}, bf16[16,8192]{1,0:T(8,128)(2,1)}), (bf16[16,2,32,128]{3,2,1,0:T(8,128)(2,1)}, bf16[16,8192]{1,0:T(8,128)(2,1)})) %all-reduce.9.cloned.1.call-update) | async-done | bytes 524304 | tf_op jit(solution)/shard_map/psum | solution.py:26
  288.5 0.0 all-gather.7.cloned.1.call-start
  288.5 45.4 %all-gather.5.cloned.1.call-done = bf16[256,8192]{1,0:T(8,128)(2,1)} async-done(((bf16[16,8192]{1,0:T(8,128)(2,1)}), bf16[256,8192]{1,0:T(8,128)(2,1)}) %all-gather.5.cloned.1.call-update) | async-done | bytes 4194320 | tf_op jit(solution)/shard_map/all_gather | solution.py:108
  333.9 3.7 convert_reduce_fusion.1
  337.6 0.0 reduce-scatter.15.cloned.1.call-start
  337.6 40.8 %all-gather.7.cloned.1.call-done = bf16[256,8192]{1,0:T(8,128)(2,1)} async-done(((bf16[16,8192]{1,0:T(8,128)(2,1)}), bf16[256,8192]{1,0:T(8,128)(2,1)}) %all-gather.7.cloned.1.call-update) | async-done | bytes 4194320 | tf_op jit(solution)/shard_map/all_gather | solution.py:117
  378.4 16.1 %fusion.24 = (f32[128]{0:T(128)S(1)}, f32[128]{0:T(128)S(1)}, f32[128]{0:T(128)S(1)}, f32[128]{0:T(128)S(1)}, f32[128]{0:T(128)S(1)}, /*index=5*/f32[128]{0:T(12...) fusion(s32[]{:T(128)S(6)} %select_n.96, s32[]{:T(128)S(6)} %select_n.95, ...), kind=kOutput, calls=%fused_computation.64 | convolution fusion | flops 567278464 | bytes 8458768 | tf_op jit(solution)/shard_map/dot_general | solution.py:119
  394.5 16.2 %fusion.15 = f32[2,32,128,128]{3,2,1,0:T(8,128)S(1)} fusion(bf16[2,32,128,128]{3,2,1,0:T(8,128)(2,1)S(1)} %bitcast.127, s32[]{:T(128)S(6)} %select_n.96, s32[]{:T(128)S(6)} %select_n.95, s32[]{:T(128)S(6)} %select_n.94, s32[]{:T(128)S(6)} %select_n.93, f32[128]{0:T(128)S(1)} %get-tuple-element.153, f32[128]{0:T(128)S(1)} %get-tuple-element.154, ...), kind=kLoop, calls=%fused_computation.55 | loop fusion | flops 27262976 | bytes 6296080 | tf_op jit(solution)/shard_map/add | solution.py:138
  410.7 0.3 copy.37
  411.0 4.4 copy.50
  415.4 0.3 all-reduce.7.cloned.1.call-start
  415.7 0.6 copy-done.3
  416.3 0.2 convert_reduce_fusion
  416.5 3.4 fusion.26
  420.0 17.6 %all-reduce.2 = (f32[1,9,128]{2,1,0:T(8,128)S(1)}, f32[1,16]{1,0:T(1,128)}, f32[1,16,256]{2,1,0:T(8,128)}, f32[16]{0:T(128)}) all-reduce(f32[1,9,128]{2,1,0:T(8,128)S(1)} %bitcast.132, f32[1,16]{1,0:T(1,128)S(1)} %multiply_bitcast_fusion, f32[1,16,256]{2,1,0:T(8,128)S(1)} %fusion.26, ...), channel_id=1, replica_groups=mesh['section'=4,'dp'=4,'chan'=16] {'dp'}, use_global_device_ids=true, to_apply=%region_16.17 | all-reduce | flops 5280 | bytes 42240 | tf_op jit(solution)/shard_map/psum | solution.py:144
  437.7 0.6 copy.32
  438.3 4.5 fusion.25
  442.8 18.3 %reduce-scatter.15.cloned.1.call-done = f32[8,32768]{1,0:T(8,128)} async-done(((f32[32,32768]{1,0:T(8,128)}), f32[8,32768]{1,0:T(8,128)}) %reduce-scatter.15.cloned.1.call-update) | async-done | bytes 1048592
  461.1 1.4 copy.42
  462.5 1.0 fusion.27
  463.5 47.9 %all-reduce.7.cloned.1.call-done = f32[1,128,256]{2,1,0:T(8,128)} async-done(((f32[1,128,256]{2,1,0:T(8,128)}), f32[1,128,256]{2,1,0:T(8,128)}) %all-reduce.7.cloned.1.call-update) | async-done | bytes 131088 | tf_op jit(solution)/shard_map/psum | solution.py:144
  511.4 0.7 copy.60
  512.1 1.6 copy.61
  (37 shorter events, 0.3 us)
Async XLA Ops:
  7.2 20.7 %copy-start = (bf16[1,128,256]{2,1,0:T(8,128)(2,1)S(1)}, bf16[1,128,256]{2,1,0:T(8,128)(2,1)}, u32[]{:S(2)}) copy-start(bf16[1,128,256]{2,1,0:T(8,128)(2,1)} %param.17) | copy-start | bytes 196612
  7.2 107.7 %reduce-scatter.11.cloned.1.call-start = ((), (), s32[]{:S(2)}) async-start(), calls=%async_computation.7 | async-start | bytes 8912896 | tf_op jit(solution)/shard_map/reduce_scatter | solution.py:75
  10.5 1.4 copy-start.1
  41.2 73.7 %copy-start.7 = (bf16[1,16,256]{2,1,0:T(8,128)(2,1)S(1)}, bf16[1,16,256]{2,1,0:T(8,128)(2,1)}, u32[]{:S(2)}) copy-start(bf16[1,16,256]{2,1,0:T(8,128)(2,1)} %param.19) | copy-start | bytes 24580
  41.2 73.7 %copy-start.8 = (f32[1,16]{1,0:T(1,128)S(1)}, f32[1,16]{1,0:T(1,128)}, u32[]{:S(2)}) copy-start(f32[1,16]{1,0:T(1,128)} %param.18) | copy-start | bytes 196
  41.2 157.7 %reduce-scatter.13.cloned.1.call-start = ((), (), s32[]{:S(2)}) async-start(), calls=%async_computation.8 | async-start | bytes 8912896 | tf_op jit(solution)/shard_map/reduce_scatter | solution.py:88
  129.5 69.5 %copy-start.4 = (bf16[16,2,32,128]{3,2,1,0:T(8,128)(2,1)S(1)}, bf16[16,2,32,128]{3,2,1,0:T(8,128)(2,1)}, u32[]{:S(2)}) copy-start(bf16[16,2,32,128]{3,2,1,0:T(8,128)(2,1)} %param.21) | copy-start | bytes 786436
  129.5 70.4 %copy-start.6 = (s32[2,32,128]{2,1,0:T(8,128)S(1)}, s32[2,32,128]{2,1,0:T(8,128)}, u32[]{:S(2)}) copy-start(s32[2,32,128]{2,1,0:T(8,128)} %param.15) | copy-start | bytes 98308
  129.5 102.5 %all-gather.9.cloned.1.call-start = ((), (), s32[]{:S(2)}) async-start(), calls=%async_computation.6 | async-start | bytes 2621440 | tf_op jit(solution)/shard_map/all_gather | solution.py:13
  199.0 89.5 %all-reduce.9.cloned.1.call-start = ((), (), s32[]{:S(2)}) async-start(), calls=%async_computation.10 | async-start | bytes 1048576 | tf_op jit(solution)/shard_map/psum | solution.py:26
  199.9 37.0 %copy-start.9 = (f32[16]{0:T(128)S(1)}, f32[16]{0:T(128)}, u32[]{:S(2)}) copy-start(f32[16]{0:T(128)} %param.20) | copy-start | bytes 196
  232.0 101.9 %copy-start.2 = (f32[16,8192]{1,0:T(8,128)S(1)}, f32[16,8192]{1,0:T(8,128)}, u32[]{:S(2)}) copy-start(f32[16,8192]{1,0:T(8,128)} %reduce-scatter.11.cloned.1.call-done) | copy-start | bytes 1572868
  240.1 93.8 %all-gather.5.cloned.1.call-start = ((), (), s32[]{:S(2)}) async-start(), calls=%async_computation.3 | async-start | bytes 4456448 | tf_op jit(solution)/shard_map/all_gather | solution.py:108
  288.5 90.0 %all-gather.7.cloned.1.call-start = ((), (), s32[]{:S(2)}) async-start(), calls=%async_computation.4 | async-start | bytes 4456448 | tf_op jit(solution)/shard_map/all_gather | solution.py:117
  337.6 123.5 %reduce-scatter.15.cloned.1.call-start = ((), (), s32[]{:S(2)}) async-start(), calls=%async_computation.9 | async-start | bytes 5242880
  415.4 0.9 copy-start.3
  415.4 95.9 %all-reduce.7.cloned.1.call-start = ((), (), s32[]{:S(2)}) async-start(), calls=%async_computation.5 | async-start | bytes 262144 | tf_op jit(solution)/shard_map/psum | solution.py:144
  438.3 73.1 %copy-start.5 = (bf16[16,2,32,128]{3,2,1,0:T(8,128)(2,1)S(1)}, bf16[16,2,32,128]{3,2,1,0:T(8,128)(2,1)}, u32[]{:S(2)}) copy-start(bf16[16,2,32,128]{3,2,1,0:T(8,128)(2,1)} %get-tuple-element.217) | copy-start | bytes 786436
Sparse Core Ops, SparseCore 0:
  41.4 73.4 reduce-scatter.10
  129.6 69.2 reduce-scatter.12
  200.8 31.1 all-gather.8
  240.2 48.1 all-reduce.8
  290.1 43.7 all-gather.4
  337.7 40.6 all-gather.6
  415.5 45.4 reduce-scatter.14
  464.0 47.2 all-reduce.6
where the time goes:
time: 521 us; the launch traced here: 520 us
  waiting for transfers between devices  376 us (72%)
  other arithmetic  44.7 us (9%)
  matrix products  37.7 us (7%)
  local copies, waits for them, and re-layouts  29.6 us (6%)
  blocking collectives  17.6 us (3%)
  between operations  14.3 us (3%)
    reduce_scatter x1, waiting for transfers between devices, local(): lax.psum_scatter(lax.dot_general(columns, depth_rows, (((0,), (1,)), ((),...  73.4 us
    reduce_scatter x1, waiting for transfers between devices, local(): lax.psum_scatter(lax.dot_general(columns, branch_act, (((0,), (0,)), ((),...  69.4 us
    psum x1, waiting for transfers between devices, spread(): return lax.psum(kept, axis)  48.3 us
    psum x1, waiting for transfers between devices, local(): lax.psum((kernel_grad, weight_grad * scaling, pw_bias_grad, proj_grad * s...  47.9 us
    all_gather x1, waiting for transfers between devices, local(): shard_rows = lax.all_gather(out_grad, 'chan', axis=0, tiled=True)  45.4 us
    all_gather x1, waiting for transfers between devices, local(): shard_rows = lax.all_gather(pre_grad, 'chan', axis=0, tiled=True)  40.8 us
    all_gather x1, waiting for transfers between devices, prefix(): everything = lax.all_gather(shard, axis)  32.1 us
    unnamed x29, local copies, waits for them, and re-layouts  29.6 us
  transfers between devices with their start and end apart: 8, of which 8 were waited for; matrix products, arithmetic and copies ran while one was open for 2% of the time, Pallas kernels for 0%

commit v1 on v0

--- a/solution.py
+++ b/solution.py
@@ -23,7 +23,7 @@
 
 def spread(value, axis, source):
     kept = jnp.where(lax.axis_index(axis) == source, value, 0).astype(value.dtype)
-    return lax.psum(kept, axis)
+    return jnp.sum(lax.all_gather(kept, axis), axis=0)
 
 
 def column_band(offsets, widths, col_count):

time: 521 us -> 498 us (0.956)
  waiting for transfers between devices: 376 us -> 351 us
    psum x1 -> x0, waiting for transfers between devices: 48.3 us -> none  [spread(): return lax.psum(kept, axis)]
    all_gather x0 -> x2, waiting for transfers between devices: none -> 26.7 us  [spread(): return jnp.sum(lax.all_gather(kept, axis), axis=0)]
    unnamed x29 -> x26, local copies, waits for them, and re-layouts: 29.6 us -> 28.3 us
    unnamed x9 -> x10, waiting for transfers between devices: 18.4 us -> 17.6 us
  transfers between devices with their start and end apart: 8 -> 9, of which waited for: 8 -> 8; matrix products, arithmetic and copies ran while one was open for 2% -> 10% of each run, Pallas kernels for 0% -> 0%
where the time goes in v1:
time: 498 us; the launch traced here: 497 us
  waiting for transfers between devices  351 us (70%)
  other arithmetic  48.4 us (10%)
  matrix products  37.6 us (8%)
  local copies, waits for them, and re-layouts  28.3 us (6%)
  blocking collectives  17.6 us (4%)
  between operations  14 us (3%)
    reduce_scatter x1, waiting for transfers between devices, local(): lax.psum_scatter(lax.dot_general(columns, depth_rows, (((0,), (1,)), ((),...  73.3 us
    reduce_scatter x1, waiting for transfers between devices, local(): lax.psum_scatter(lax.dot_general(columns, branch_act, (((0,), (0,)), ((),...  69.5 us
    psum x1, waiting for transfers between devices, local(): lax.psum((kernel_grad, weight_grad * scaling, pw_bias_grad, proj_grad * s...  47.9 us
    all_gather x1, waiting for transfers between devices, local(): shard_rows = lax.all_gather(out_grad, 'chan', axis=0, tiled=True)  43.5 us
    all_gather x1, waiting for transfers between devices, local(): shard_rows = lax.all_gather(pre_grad, 'chan', axis=0, tiled=True)  40 us
    all_gather x1, waiting for transfers between devices, prefix(): everything = lax.all_gather(shard, axis)  32.1 us
    unnamed x26, local copies, waits for them, and re-layouts  28.3 us
    all_gather x2, waiting for transfers between devices, spread(): return jnp.sum(lax.all_gather(kept, axis), axis=0)  26.7 us
  transfers between devices with their start and end apart: 9, of which 8 were waited for; matrix products, arithmetic and copies ran while one was open for 10% of the time, Pallas kernels for 0%

profile of v1, /device:TPU:2, one launch (start us, length us, event | category | flops | bytes accessed | tf_op | source)
XLA Modules:
  0.0 497.5 jit_solution(11057854716876976411)
XLA Ops:
  7.2 0.7 convert_element_type.139
  7.9 0.7 fusion.37
  8.7 1.8 broadcast_multiply_fusion
  10.5 1.3 copy-done.1
  11.8 16.0 %fusion.10 = bf16[2,32,128,128]{3,2,1,0:T(8,128)(2,1)S(1)} fusion(bf16[2,32,128,128]{3,2,1,0:T(8,128)(2,1)S(1)} %broadcast_multiply_fusion, f32[128]{0:T(128)S(1)} %get-tuple-element.158, f32[128]{0:T(128)S(1)} %get-tuple-element.159, f32[128]{0:T(128)S(1)} %get-tuple-element.160, f32[128]{0:T(128)S(1)} %get-tuple-element.161, ...), kind=kLoop, calls=%fused_computation.50 | loop fusion | flops 28311552 | bytes 4198928 | tf_op jit(solution)/shard_map/convert_element_type | solution.py:69
  27.8 4.5 convolution_bitcast_fusion.1
  32.3 8.9 %copy.37 = f32[256,8192]{1,0:T(8,128)} copy(f32[256,8192]{0,1:T(8,128)} %convolution_bitcast_fusion.1) | data formatting | bytes 16777216
  41.2 0.2 reduce-scatter.13.cloned.1.call-start
  41.5 73.3 %reduce-scatter.11.cloned.1.call-done = f32[16,8192]{1,0:T(8,128)} async-done(((f32[256,8192]{1,0:T(8,128)}), f32[16,8192]{1,0:T(8,128)}) %reduce-scatter.11.cloned.1.call-update) | async-done | bytes 524304 | tf_op jit(solution)/shard_map/reduce_scatter | solution.py:75
  114.8 5.6 %convolution_bitcast_fusion = f32[256,8192]{0,1:T(8,128)} fusion(bf16[1,16,256]{2,1,0:T(8,128)(2,1)S(1)} %copy-done.6, f32[16,8192]{1,0:T(8,128)} %reduce-scatter.11.cloned.1.call-done, f32[16]{0:T(128)S(1)} %bitcast.137), kind=kOutput, calls=%fused_computation.27 | convolution fusion | flops 67895296 | bytes 8921152 | tf_op jit(solution)/shard_map/dot_general | solution.py:89
  120.5 8.9 %copy.39 = f32[256,8192]{1,0:T(8,128)} copy(f32[256,8192]{0,1:T(8,128)} %convolution_bitcast_fusion) | data formatting | bytes 16777216
  129.4 0.0 all-gather.13.cloned.1.call-start
  129.5 69.5 %reduce-scatter.13.cloned.1.call-done = f32[16,8192]{1,0:T(8,128)} async-done(((f32[256,8192]{1,0:T(8,128)}), f32[16,8192]{1,0:T(8,128)}) %reduce-scatter.13.cloned.1.call-update) | async-done | bytes 524304 | tf_op jit(solution)/shard_map/reduce_scatter | solution.py:88
  199.0 0.0 all-gather.17.cloned.1.call-start
  199.0 0.8 convert.4
  199.9 32.1 %all-gather.13.cloned.1.call-done = f32[64,8192]{1,0:T(8,128)} async-done(((f32[16,8192]{1,0:T(8,128)}), f32[64,8192]{1,0:T(8,128)}) %all-gather.13.cloned.1.call-update) | async-done | bytes 2097168 | tf_op jit(solution)/shard_map/all_gather | solution.py:13
  232.0 4.9 while.14
  232.0 1.3 add_select_fusion.2
  233.3 1.2 add_select_fusion.2
  234.5 1.2 add_select_fusion.2
  235.7 1.2 add_select_fusion.2
  237.0 2.5 broadcast_select_fusion
  239.4 0.0 all-gather.9.cloned.1.call-start
  239.5 26.7 %all-gather.17.cloned.1.call-done = bf16[64,8192]{1,0:T(8,128)(2,1)} async-done(((bf16[16,8192]{1,0:T(8,128)(2,1)}), bf16[64,8192]{1,0:T(8,128)(2,1)}) %all-gather.17.cloned.1.call-update) | async-done | bytes 1048592 | tf_op jit(solution)/shard_map/all_gather | solution.py:26
  266.2 2.1 reduce_sum.124
  268.4 0.0 all-gather.11.cloned.1.call-start
  268.4 43.5 %all-gather.9.cloned.1.call-done = bf16[256,8192]{1,0:T(8,128)(2,1)} async-done(((bf16[16,8192]{1,0:T(8,128)(2,1)}), bf16[256,8192]{1,0:T(8,128)(2,1)}) %all-gather.9.cloned.1.call-update) | async-done | bytes 4194320 | tf_op jit(solution)/shard_map/all_gather | solution.py:108
  311.9 3.7 convert_reduce_fusion.1
  315.6 0.0 all-gather.15.cloned.1.call-start
  315.6 0.7 all-gather.15.cloned.1.call-update
  316.4 40.0 %all-gather.11.cloned.1.call-done = bf16[256,8192]{1,0:T(8,128)(2,1)} async-done(((bf16[16,8192]{1,0:T(8,128)(2,1)}), bf16[256,8192]{1,0:T(8,128)(2,1)}) %all-gather.11.cloned.1.call-update) | async-done | bytes 4194320 | tf_op jit(solution)/shard_map/all_gather | solution.py:117
  356.4 16.1 %fusion.24 = (f32[128]{0:T(128)S(1)}, f32[128]{0:T(128)S(1)}, f32[128]{0:T(128)S(1)}, f32[128]{0:T(128)S(1)}, f32[128]{0:T(128)S(1)}, /*index=5*/f32[128]{0:T(12...) fusion(s32[]{:T(128)S(6)} %select_n.96, s32[]{:T(128)S(6)} %select_n.95, ...), kind=kOutput, calls=%fused_computation.64 | convolution fusion | flops 567278464 | bytes 8458768 | tf_op jit(solution)/shard_map/dot_general | solution.py:119
  372.5 16.2 %fusion.15 = f32[2,32,128,128]{3,2,1,0:T(8,128)S(1)} fusion(bf16[2,32,128,128]{3,2,1,0:T(8,128)(2,1)S(1)} %bitcast.128, s32[]{:T(128)S(6)} %select_n.96, s32[]{:T(128)S(6)} %select_n.95, s32[]{:T(128)S(6)} %select_n.94, s32[]{:T(128)S(6)} %select_n.93, f32[128]{0:T(128)S(1)} %get-tuple-element.158, f32[128]{0:T(128)S(1)} %get-tuple-element.159, ...), kind=kLoop, calls=%fused_computation.55 | loop fusion | flops 27262976 | bytes 6296080 | tf_op jit(solution)/shard_map/add | solution.py:138
  388.7 0.3 copy.41
  389.0 4.4 copy.54
  393.4 0.3 all-reduce.5.cloned.1.call-start
  393.7 1.5 reduce_sum.123
  395.2 0.8 copy.43
  396.0 0.2 convert_reduce_fusion
  396.2 3.4 fusion.26
  399.7 17.6 %all-reduce.2 = (f32[1,9,128]{2,1,0:T(8,128)S(1)}, f32[1,16]{1,0:T(1,128)}, f32[1,16,256]{2,1,0:T(8,128)}, f32[16]{0:T(128)}) all-reduce(f32[1,9,128]{2,1,0:T(8,128)S(1)} %bitcast.136, f32[1,16]{1,0:T(1,128)S(1)} %multiply_bitcast_fusion, f32[1,16,256]{2,1,0:T(8,128)S(1)} %fusion.26, ...), channel_id=1, replica_groups=mesh['section'=4,'dp'=4,'chan'=16] {'dp'}, use_global_device_ids=true, to_apply=%region_16.17 | all-reduce | flops 5280 | bytes 42240 | tf_op jit(solution)/shard_map/psum | solution.py:144
  417.3 0.6 copy.36
  417.9 4.4 fusion.25
  422.3 16.8 %reduce-scatter.15.cloned.1.call-done = f32[8,32768]{1,0:T(8,128)} async-done(((f32[32,32768]{1,0:T(8,128)}), f32[8,32768]{1,0:T(8,128)}) %reduce-scatter.15.cloned.1.call-update) | async-done | bytes 1048592
  439.1 1.4 copy.46
  440.5 1.0 fusion.27
  441.5 47.9 %all-reduce.5.cloned.1.call-done = f32[1,128,256]{2,1,0:T(8,128)} async-done(((f32[1,128,256]{2,1,0:T(8,128)}), f32[1,128,256]{2,1,0:T(8,128)}) %all-reduce.5.cloned.1.call-update) | async-done | bytes 131088 | tf_op jit(solution)/shard_map/psum | solution.py:144
  489.4 1.6 copy.62
  (39 shorter events, 0.4 us)
Async XLA Ops:
  7.2 20.7 %copy-start = (bf16[1,128,256]{2,1,0:T(8,128)(2,1)S(1)}, bf16[1,128,256]{2,1,0:T(8,128)(2,1)}, u32[]{:S(2)}) copy-start(bf16[1,128,256]{2,1,0:T(8,128)(2,1)} %param.17) | copy-start | bytes 196612
  7.2 107.6 %reduce-scatter.11.cloned.1.call-start = ((), (), s32[]{:S(2)}) async-start(), calls=%async_computation.9 | async-start | bytes 8912896 | tf_op jit(solution)/shard_map/reduce_scatter | solution.py:75
  10.5 1.4 copy-start.1
  41.2 73.6 %copy-start.6 = (bf16[1,16,256]{2,1,0:T(8,128)(2,1)S(1)}, bf16[1,16,256]{2,1,0:T(8,128)(2,1)}, u32[]{:S(2)}) copy-start(bf16[1,16,256]{2,1,0:T(8,128)(2,1)} %param.19) | copy-start | bytes 24580
  41.2 73.6 %copy-start.7 = (f32[1,16]{1,0:T(1,128)S(1)}, f32[1,16]{1,0:T(1,128)}, u32[]{:S(2)}) copy-start(f32[1,16]{1,0:T(1,128)} %param.18) | copy-start | bytes 196
  41.2 157.7 %reduce-scatter.13.cloned.1.call-start = ((), (), s32[]{:S(2)}) async-start(), calls=%async_computation.10 | async-start | bytes 8912896 | tf_op jit(solution)/shard_map/reduce_scatter | solution.py:88
  129.4 69.6 %copy-start.4 = (bf16[16,2,32,128]{3,2,1,0:T(8,128)(2,1)S(1)}, bf16[16,2,32,128]{3,2,1,0:T(8,128)(2,1)}, u32[]{:S(2)}) copy-start(bf16[16,2,32,128]{3,2,1,0:T(8,128)(2,1)} %param.21) | copy-start | bytes 786436
  129.4 70.5 %copy-start.5 = (s32[2,32,128]{2,1,0:T(8,128)S(1)}, s32[2,32,128]{2,1,0:T(8,128)}, u32[]{:S(2)}) copy-start(s32[2,32,128]{2,1,0:T(8,128)} %param.15) | copy-start | bytes 98308
  129.4 102.6 %all-gather.13.cloned.1.call-start = ((), (), s32[]{:S(2)}) async-start(), calls=%async_computation.6 | async-start | bytes 2621440 | tf_op jit(solution)/shard_map/all_gather | solution.py:13
  199.0 67.2 %all-gather.17.cloned.1.call-start = ((), (), s32[]{:S(2)}) async-start(), calls=%async_computation.8 | async-start | bytes 1310720 | tf_op jit(solution)/shard_map/all_gather | solution.py:26
  199.9 37.1 %copy-start.8 = (f32[16]{0:T(128)S(1)}, f32[16]{0:T(128)}, u32[]{:S(2)}) copy-start(f32[16]{0:T(128)} %param.20) | copy-start | bytes 196
  232.0 79.9 %copy-start.2 = (f32[16,8192]{1,0:T(8,128)S(1)}, f32[16,8192]{1,0:T(8,128)}, u32[]{:S(2)}) copy-start(f32[16,8192]{1,0:T(8,128)} %reduce-scatter.11.cloned.1.call-done) | copy-start | bytes 1572868
  239.4 72.4 %all-gather.9.cloned.1.call-start = ((), (), s32[]{:S(2)}) async-start(), calls=%async_computation.3 | async-start | bytes 4456448 | tf_op jit(solution)/shard_map/all_gather | solution.py:108
  268.4 88.0 %all-gather.11.cloned.1.call-start = ((), (), s32[]{:S(2)}) async-start(), calls=%async_computation.4 | async-start | bytes 4456448 | tf_op jit(solution)/shard_map/all_gather | solution.py:117
  315.6 78.2 %all-gather.15.cloned.1.call-start = ((), (), s32[]{:S(2)}) async-start(), calls=%async_computation.7 | async-start | bytes 1310720 | tf_op jit(solution)/shard_map/all_gather | solution.py:26
  316.3 122.7 %reduce-scatter.15.cloned.1.call-start = ((), (), s32[]{:S(2)}) async-start(), calls=%async_computation.11 | async-start | bytes 5242880
  393.4 2.6 copy-start.3
  393.4 95.9 %all-reduce.5.cloned.1.call-start = ((), (), s32[]{:S(2)}) async-start(), calls=%async_computation.5 | async-start | bytes 262144 | tf_op jit(solution)/shard_map/psum | solution.py:144
Sparse Core Ops, SparseCore 0:
  41.4 73.4 reduce-scatter.10
  129.6 69.3 reduce-scatter.12
  200.8 31.2 all-gather.12
  239.6 26.5 all-gather.16
  268.5 43.3 all-gather.8
  315.7 40.6 all-gather.10
  358.2 24.1 all-gather.14
  393.5 45.4 reduce-scatter.14
  442.1 47.2 all-reduce.4
